TPU v7x, 32 devices: a whole 2x2x4 slice. The times are simulated.
32 devices in a mesh: kv: 2 (over y), ctx: 16 (over z, x, core).
Axes of the slice: x: 2, y: 2, z: 4, core: 2. Of those that a mesh axis runs over, the one named last changes fastest.
Arguments:
- residual: bfloat16 [64, 8192], P(None, 'ctx'), may hold values from -8 to 8
- queries: bfloat16 [64, 8192], P(None, 'kv'), may hold values from -16 to 16
- draft_token_keys: bfloat16 [64, 1024], P(None, 'kv'), may hold values from -32 to 32
- draft_token_values: bfloat16 [64, 1024], P(None, 'kv'), may hold values from -8 to 8
- cache_keys: bfloat16 [2, 8192, 1024], P(None, 'ctx', 'kv'), may hold values from -32 to 32
- cached_value_rows: bfloat16 [2, 8192, 1024], P(None, 'ctx', 'kv'), may hold values from -8 to 8
- tenant_ids: int32 [64], replicated, may hold values from 0 to 1, as said below
- tree_mask: int32 [64, 64], replicated, may hold values from 0 to 1, as said below
- cache_lengths: int32 [2], replicated, may hold values from 4097 to 8192
- out_weight: bfloat16 [8192, 8192], P('kv', 'ctx'), may hold values from -0.0625 to 0.0625
- out_signs: bfloat16 [2, 8192, 8192], P(None, 'kv', 'ctx'), may hold values from -1 to 1, as said below
- norm_gain: float32 [8192], P('ctx'), may hold values from 0.1 to 1.9
- gate_weight: bfloat16 [8192, 16384], P(None, ('kv', 'ctx')), may hold values from -0.0625 to 0.0625
- up_weight: bfloat16 [8192, 16384], P(None, ('kv', 'ctx')), may hold values from -0.0625 to 0.0625
- down_weight: bfloat16 [16384, 8192], P(('kv', 'ctx')), may hold values from -0.09375 to 0.09375
- gate_signs: bfloat16 [2, 8192, 16384], P(None, None, ('kv', 'ctx')), may hold values from -1 to 1, as said below
- up_signs: bfloat16 [2, 8192, 16384], P(None, None, ('kv', 'ctx')), may hold values from -1 to 1, as said below
- down_signs: bfloat16 [2, 16384, 8192], P(None, ('kv', 'ctx')), may hold values from -1 to 1, as said below
- delta_scale: float32 [2, 4], replicated, may hold values from 0.3 to 0.9
Outputs:
- mixed: bfloat16 [64, 8192], P(None, 'ctx')
Inputs may be any that keep to these rules, and one draw needn't show every extreme that they name: `tenant_ids`: exactly 32 tokens belong to each tenant. `tree_mask`: entry (i, j) is 1 exactly when token j is token i or an ancestor of token i in the draft tree of their common tenant; each tenant's 32 tokens form one tree. `out_signs`: every entry is 1 or -1. `gate_signs`: every entry is 1 or -1. `up_signs`: every entry is 1 or -1. `down_signs`: every entry is 1 or -1.
All inputs are finite; a program needn't handle non-finite values.
Results may differ from a plain program's by a relative error of at most 0.013.
Values may be sent and summed in bfloat16 or wider, within the bound.
No kernel may reach another device: no remote copies, remote signals or barrier semaphores. Data moves between devices by JAX's collectives and lax.ppermute only.
A program may use at most 192 MiB of HBM per device.

v0:
```python
import jax
import jax.numpy as jnp
from jax import lax
from jax.sharding import PartitionSpec as P

D = 8192
QUERY_HEADS = 64
HEAD_SIZE = 128
FF = 16384
NEG = -1e30
EPS = 1e-05


def combine(first, second):
    first_top, first_total, first_out = first
    second_top, second_total, second_out = second
    peak = jnp.maximum(first_top, second_top)
    first_scale = jnp.exp(first_top - peak)
    second_scale = jnp.exp(second_top - peak)
    total = first_total * first_scale + second_total * second_scale
    merged = first_out * first_scale[..., None] + second_out * second_scale[..., None]
    return (peak, total, merged)


def draft_rows(query_rows, group_rows, visible_rows, key_rows, value_rows, factor):
    groups = key_rows.shape[1]
    choose = (group_rows[:, None] == jnp.arange(groups, dtype=jnp.int32)[None, :]).astype(
        jnp.float32
    )
    every_group = (
        jnp.einsum("rd,kgd->rgk", query_rows, key_rows, preferred_element_type=jnp.float32) * factor
    )
    scores = jnp.einsum("rgk,rg->rk", every_group, choose, precision=lax.Precision.HIGHEST)
    masked = jnp.where(visible_rows, scores, NEG)
    peak = jnp.max(masked, axis=-1)
    weights = jnp.where(visible_rows, jnp.exp(masked - peak[:, None]), 0.0)
    total = jnp.sum(weights, axis=-1)
    every_value = jnp.einsum(
        "rk,kgd->rgd", weights.astype(jnp.bfloat16), value_rows, preferred_element_type=jnp.float32
    )
    result = jnp.einsum("rgd,rg->rd", every_value, choose, precision=lax.Precision.HIGHEST)
    return (peak, total, result)


def shards(
    residual,
    queries,
    draft_token_keys,
    draft_token_values,
    cache_keys,
    cached_value_rows,
    tenant_ids,
    tree_mask,
    cache_lengths,
    out_weight,
    out_signs,
    norm_gain,
    gate_weight,
    up_weight,
    down_weight,
    gate_signs,
    up_signs,
    down_signs,
    delta_scale,
):
    tenants = cache_keys.shape[0]
    tokens = tenant_ids.shape[0]
    draft = tokens // tenants
    heads_here = queries.shape[1] // HEAD_SIZE
    groups_here = draft_token_keys.shape[1] // HEAD_SIZE
    group_width = heads_here // groups_here
    ctx_rows = cache_keys.shape[1]
    factor = HEAD_SIZE ** (-0.5)
    sort_order = jnp.argsort(tenant_ids, stable=True)
    inverse = jnp.argsort(sort_order)
    sorted_queries = queries[sort_order]
    query_blocks = sorted_queries.reshape(tenants, draft, groups_here, group_width, HEAD_SIZE)
    draft_key_lines = draft_token_keys[sort_order].reshape(tokens, groups_here, HEAD_SIZE)
    draft_value_lines = draft_token_values[sort_order].reshape(tokens, groups_here, HEAD_SIZE)
    visible = tree_mask[sort_order][:, sort_order] > 0
    first_slot = lax.axis_index("ctx") * ctx_rows
    slot_ids = first_slot + jnp.arange(ctx_rows, dtype=jnp.int32)
    live = (slot_ids[None, :] < cache_lengths[:, None])[:, None, None, None, :]
    cache_key_blocks = cache_keys.reshape(tenants, ctx_rows, groups_here, HEAD_SIZE)
    cache_value_blocks = cached_value_rows.reshape(tenants, ctx_rows, groups_here, HEAD_SIZE)
    scores = (
        jnp.einsum(
            "tqgwd,tjgd->tqgwj", query_blocks, cache_key_blocks, preferred_element_type=jnp.float32
        )
        * factor
    )
    masked = jnp.where(live, scores, NEG)
    peak = jnp.max(masked, axis=-1)
    weights = jnp.where(live, jnp.exp(masked - peak[..., None]), 0.0)
    total = jnp.sum(weights, axis=-1)
    weighted = jnp.einsum(
        "tqgwj,tjgd->tqgwd",
        weights.astype(jnp.bfloat16),
        cache_value_blocks,
        preferred_element_type=jnp.float32,
    )
    part_top = peak.reshape(tokens, heads_here)
    part_total = total.reshape(tokens, heads_here)
    part_out = weighted.reshape(tokens, heads_here, HEAD_SIZE)
    n_ctx = lax.axis_size("ctx")
    all_rows = tokens * heads_here
    share = all_rows // n_ctx
    got_top, got_total, got_out = (
        lax.all_to_all(
            part_top.reshape(1, all_rows), "ctx", split_axis=1, concat_axis=0, tiled=True
        ),
        lax.all_to_all(
            part_total.reshape(1, all_rows), "ctx", split_axis=1, concat_axis=0, tiled=True
        ),
        lax.all_to_all(
            part_out.reshape(1, all_rows, HEAD_SIZE), "ctx", split_axis=1, concat_axis=0, tiled=True
        ),
    )
    summit = jnp.max(got_top, axis=0)
    rescale = jnp.exp(got_top - summit)
    merged = (
        summit,
        jnp.sum(got_total * rescale, axis=0),
        jnp.sum(got_out * rescale[..., None], axis=0),
    )
    first_row = lax.axis_index("ctx") * share
    row_ids = first_row + jnp.arange(share, dtype=jnp.int32)
    token_rows = row_ids // heads_here
    group_rows = row_ids % heads_here // group_width
    query_rows = lax.dynamic_slice_in_dim(
        sorted_queries.reshape(all_rows, HEAD_SIZE), first_row, share, 0
    )
    own = draft_rows(
        query_rows, group_rows, visible[token_rows], draft_key_lines, draft_value_lines, factor
    )
    final_top, final_total, final_out = combine(merged, own)
    finished = (final_out / final_total[:, None]).astype(jnp.bfloat16)
    attention = lax.all_gather(finished, "ctx", axis=0, tiled=True).reshape(
        tokens, heads_here * HEAD_SIZE
    )
    attention_split = attention.reshape(tenants, draft, -1)
    projected = jnp.dot(attention, out_weight, preferred_element_type=jnp.float32)
    out_delta = jnp.einsum(
        "tqh,thf->tqf", attention_split, out_signs, preferred_element_type=jnp.float32
    )
    projected = projected + (
        out_delta * (delta_scale[:, 0] * (QUERY_HEADS * HEAD_SIZE) ** (-0.5))[:, None, None]
    ).reshape(tokens, -1)
    summed_heads = lax.psum(projected.astype(jnp.bfloat16), "kv").astype(jnp.float32)
    hidden = residual[sort_order].astype(jnp.float32) + summed_heads
    squares = lax.psum(jnp.sum(hidden * hidden, axis=1), "ctx")
    normed = (hidden * lax.rsqrt(squares / D + EPS)[:, None] * norm_gain).astype(jnp.bfloat16)
    hidden_units = gate_weight.shape[1]
    piece = lax.all_gather(normed, "ctx", axis=1, tiled=True)
    size = piece.shape[1]
    split_piece = piece.reshape(tenants, draft, size)
    gate_base = jnp.dot(piece, gate_weight, preferred_element_type=jnp.float32)
    up_base = jnp.dot(piece, up_weight, preferred_element_type=jnp.float32)
    gate_delta = jnp.einsum(
        "tqf,tfh->tqh", split_piece, gate_signs, preferred_element_type=jnp.float32
    )
    up_delta = jnp.einsum("tqf,tfh->tqh", split_piece, up_signs, preferred_element_type=jnp.float32)
    gate = gate_base + (gate_delta * (delta_scale[:, 1] * D ** (-0.5))[:, None, None]).reshape(
        tokens, hidden_units
    )
    up_part = up_base + (up_delta * (delta_scale[:, 2] * D ** (-0.5))[:, None, None]).reshape(
        tokens, hidden_units
    )
    active = (jax.nn.silu(gate) * up_part).astype(jnp.bfloat16)
    active_split = active.reshape(tenants, draft, hidden_units)
    down_factor = delta_scale[:, 3] * FF ** (-0.5)
    features_here = residual.shape[1]
    base_part = lax.dot_general(
        down_weight, active, (((0,), (1,)), ((), ())), preferred_element_type=jnp.float32
    )
    delta_part = jnp.einsum(
        "thf,tqh->ftq", down_signs, active_split, preferred_element_type=jnp.float32
    )
    delta_part = delta_part * down_factor[None, :, None]
    lowered = lax.psum_scatter(
        base_part + delta_part.reshape(features_here * lax.axis_size("ctx"), tokens),
        "ctx",
        scatter_dimension=0,
        tiled=True,
    )
    lowered = lax.psum(lowered.astype(jnp.bfloat16), "kv").astype(jnp.float32)
    return (hidden + lowered.T).astype(jnp.bfloat16)[inverse]


def solution(mesh):
    return jax.shard_map(
        shards,
        mesh=mesh,
        in_specs=(
            P(None, "ctx"),
            P(None, "kv"),
            P(None, "kv"),
            P(None, "kv"),
            P(None, "ctx", "kv"),
            P(None, "ctx", "kv"),
            P(),
            P(),
            P(),
            P("kv", "ctx"),
            P(None, "kv", "ctx"),
            P("ctx"),
            P(None, ("kv", "ctx")),
            P(None, ("kv", "ctx")),
            P(("kv", "ctx"), None),
            P(None, None, ("kv", "ctx")),
            P(None, None, ("kv", "ctx")),
            P(None, ("kv", "ctx"), None),
            P(),
        ),
        out_specs=P(None, "ctx"),
        check_vma=False,
    )
```

profile of v0, /device:TPU:0, one launch (start us, length us, event | category | flops | bytes accessed | tf_op | source)
XLA Modules:
  0.0 308.4 jit_solution(11207596414709739598)
XLA Ops:
  6.5 2.8 sort.34
  9.4 0.9 gather_fusion.1
  10.4 0.3 reshape.250
  10.7 0.9 bitcast_reduce_fusion
  11.7 1.9 copy-done.3
  13.6 1.3 fusion.3
  14.9 0.8 all_to_all.38
  15.7 7.4 %all-to-all-start.2 = ((f32[1,16,128]{2,0,1:T(1,128)}), f32[1,16,128]{2,0,1:T(1,128)S(1)}, u32[]{:S(2)}, u32[]{:S(2)}) async-start(f32[1,16,128]{2,0,1:T(1,128)} %bitcast.17), calls=%async_computation.2 | async-start | bytes 16384 | tf_op jit(solution)/shard_map/all_to_all | solution.py:112
  23.1 1.1 reshape.251
  24.2 3.6 %fusion.9 = f32[2,32,4,8,128]{4,3,1,2,0:T(8,128)S(1)} fusion(f32[2,4,32,8,512]{4,3,2,1,0:T(8,128)} %copy-done.3, f32[2,32,4,8]{3,1,2,0:T(8,128)S(1)} %get-tuple-element.20, pred[2,512]{1,0:T(4,128)(4,1)S(1)} %broadcast_compare_fusion, bf16[2,512,4,128,1]{3,2,1,0,4:T(4,128)(2,1)} %bitcast.112), kind=kOutput, calls=%fused_computation.21 | convolution fusion | flops 273678336 | bytes 6300672 | tf_op jit(solution)/shard_map/tqgwj,tjgd->tqgwd/dot_general | solution.py:96
  27.9 0.7 all_to_all.35
  28.7 0.8 all-to-all-done.2
  29.4 5.2 %all-to-all-start.1 = ((f32[1,16,128]{2,0,1:T(1,128)}), f32[1,16,128]{2,0,1:T(1,128)S(1)}, u32[]{:S(2)}, u32[]{:S(2)}) async-start(f32[1,16,128]{2,0,1:T(1,128)} %bitcast.7), calls=%async_computation.1 | async-start | bytes 16384 | tf_op jit(solution)/shard_map/all_to_all | solution.py:109
  34.7 0.2 reshape.253
  35.0 1.1 copy.49
  36.1 5.0 %all-to-all-done.1 = f32[1,16,128]{2,0,1:T(1,128)S(1)} async-done(((f32[1,16,128]{2,0,1:T(1,128)}), f32[1,16,128]{2,0,1:T(1,128)S(1)}, u32[]{:S(2)}, u32[]{:S(2)}) %all-to-all-start.1) | async-done | bytes 8224 | tf_op jit(solution)/shard_map/all_to_all | solution.py:109
  41.1 3.7 %all-to-all-start = ((f32[1,2048,128]{2,0,1:T(1,128)}), f32[1,2048,128]{2,0,1:T(1,128)S(1)}, u32[]{:S(2)}, u32[]{:S(2)}) async-start(f32[1,2048,128]{2,0,1:T(1,128)} %bitcast.5), calls=%async_computation | async-start | bytes 2097152 | tf_op jit(solution)/shard_map/all_to_all | solution.py:115
  45.0 0.7 gather_fusion.5
  45.7 0.6 gather_fusion.2
  46.4 0.6 gather_fusion.3
  47.2 0.7 gather_fusion.4
  47.9 0.7 gather_fusion.6
  49.3 0.7 fusion.22
  50.1 17.5 %all-to-all-done = f32[1,2048,128]{2,0,1:T(1,128)S(1)} async-done(((f32[1,2048,128]{2,0,1:T(1,128)}), f32[1,2048,128]{2,0,1:T(1,128)S(1)}, u32[]{:S(2)}, u32[]{:S(2)}) %all-to-all-start) | async-done | bytes 1048608 | tf_op jit(solution)/shard_map/all_to_all | solution.py:115
  67.6 0.3 multiply_reduce_fusion
  68.1 24.0 %all_gather.6 = bf16[2048,128]{1,0:T(8,128)(2,1)S(1)} all-gather(bf16[128,128]{1,0:T(8,128)(2,1)S(1)} %divide_convert_fusion), channel_id=1, replica_groups=mesh['kv'=2,'ctx'=16] {'ctx'}, dimensions={0}, use_global_device_ids=true | all-gather | bytes 557056 | tf_op jit(solution)/shard_map/all_gather | solution.py:138
  92.6 5.1 %convolution_multiply_fusion.1 = f32[2,32,512]{2,1,0:T(8,128)S(1)} fusion(bf16[2,32,4096]{2,1,0:T(8,128)(2,1)S(1)} %reshape_reshape.9, bf16[2,4096,512]{2,1,0:T(8,128)(2,1)} %param.29, f32[2]{0:T(128)S(1)} %get-tuple-element.11), kind=kOutput, calls=%fused_computation.22 | convolution fusion | flops 268468224 | bytes 9043976 | tf_op jit(solution)/shard_map/tqh,thf->tqf/dot_general | solution.py:143
  97.6 1.5 fusion.16
  99.2 0.7 gather_fusion
  99.9 17.6 %all-reduce.3.cloned.1.call-done = bf16[64,512]{1,0:T(8,128)(2,1)} async-done(((bf16[64,512]{1,0:T(8,128)(2,1)}), bf16[64,512]{1,0:T(8,128)(2,1)}) %all-reduce.3.cloned.1.call-update) | async-done | bytes 65552 | tf_op jit(solution)/shard_map/psum | solution.py:149
  117.5 1.0 multiply_reduce_fusion.1
  118.5 32.7 %psum.22 = f32[64]{0:T(128)S(1)} all-reduce(f32[64]{0:T(128)S(1)} %multiply_reduce_fusion.1), channel_id=1, replica_groups=mesh['kv'=2,'ctx'=16] {'ctx'}, use_global_device_ids=true, to_apply=%region_10.11 | all-reduce | flops 64 | bytes 512 | tf_op jit(solution)/shard_map/psum | solution.py:151
  151.2 1.6 multiply_convert_fusion
  153.0 32.9 %all-gather.2.cloned.1.call-done = bf16[64,8192]{1,0:T(8,128)(2,1)} async-done(((bf16[64,512]{1,0:T(8,128)(2,1)}), bf16[64,8192]{1,0:T(8,128)(2,1)}) %all-gather.2.cloned.1.call-update) | async-done | bytes 1048592 | tf_op jit(solution)/shard_map/all_gather | solution.py:154
  185.9 9.1 %convolution_multiply_fusion.3 = f32[2,32,512]{2,1,0:T(8,128)S(1)} fusion(bf16[2,32,8192]{2,1,0:T(8,128)(2,1)} %bitcast.93, bf16[2,8192,512]{2,1,0:T(8,128)(2,1)} %param.34, f32[2]{0:T(128)S(1)} %get-tuple-element.10), kind=kOutput, calls=%fused_computation.27 | convolution fusion | flops 536903680 | bytes 17956872 | tf_op jit(solution)/shard_map/tqf,tfh->tqh/dot_general | solution.py:159
  195.1 8.8 %convolution_multiply_fusion.2 = f32[2,32,512]{2,1,0:T(8,128)S(1)} fusion(bf16[2,32,8192]{2,1,0:T(8,128)(2,1)S(1)} %bitcast.94, bf16[2,8192,512]{2,1,0:T(8,128)(2,1)} %param.35, f32[2]{0:T(128)S(1)} %get-tuple-element.12), kind=kOutput, calls=%fused_computation.24 | convolution fusion | flops 536903680 | bytes 17956872 | tf_op jit(solution)/shard_map/tqf,tfh->tqh/dot_general | solution.py:162
  204.0 1.6 convolution_add_fusion.2
  205.7 1.6 fusion.15
  207.5 1.2 slice-done.8
  208.7 1.4 slice-done.9
  210.1 3.0 convolution_multiply_fusion
  213.1 2.9 fusion
  216.1 2.0 sort.35
  218.1 59.5 %reduce-scatter.2.cloned.1.call-done = f32[512,64]{0,1:T(8,128)} async-done(((f32[8192,64]{0,1:T(8,128)}), f32[512,64]{0,1:T(8,128)}) %reduce-scatter.2.cloned.1.call-update) | async-done | bytes 131088 | tf_op jit(solution)/shard_map/reduce_scatter | solution.py:180
  277.7 1.5 convert_bitcast_fusion
  279.3 20.4 %all-reduce.5.cloned.1.call-done = bf16[64,512]{1,0:T(8,128)(2,1)} async-done(((bf16[64,512]{1,0:T(8,128)(2,1)}), bf16[64,512]{1,0:T(8,128)(2,1)}) %all-reduce.5.cloned.1.call-update) | async-done | bytes 65552 | tf_op jit(solution)/shard_map/psum | solution.py:186
  299.7 0.9 add_convert_fusion
  300.6 1.3 gather_fusion.7
  (91 shorter events, 3.0 us)
Async XLA Ops:
  6.5 2.8 copy-start
  6.5 3.8 %copy-start.9 = (bf16[2,512,512]{2,1,0:T(8,128)(2,1)S(1)}, bf16[2,512,512]{2,1,0:T(8,128)(2,1)}, u32[]{:S(2)}) copy-start(bf16[2,512,512]{2,1,0:T(8,128)(2,1)} %param.23) | copy-start | bytes 3145732
  6.5 4.1 %copy-start.14 = (s32[2]{0:T(128)S(1)}, s32[2]{0:T(128)}, u32[]{:S(2)}) copy-start(s32[2]{0:T(128)} %param.27) | copy-start | bytes 28
  10.7 12.3 %copy-start.10 = (bf16[2,512,512]{2,1,0:T(8,128)(2,1)S(1)}, bf16[2,512,512]{2,1,0:T(8,128)(2,1)}, u32[]{:S(2)}) copy-start(bf16[2,512,512]{2,1,0:T(8,128)(2,1)} %param.24) | copy-start | bytes 3145732
  11.6 1.9 copy-start.3
  15.7 13.8 %all-to-all-start.2 = ((f32[1,16,128]{2,0,1:T(1,128)}), f32[1,16,128]{2,0,1:T(1,128)S(1)}, u32[]{:S(2)}, u32[]{:S(2)}) async-start(f32[1,16,128]{2,0,1:T(1,128)} %bitcast.17), calls=%async_computation.2 | async-start | bytes 16384 | tf_op jit(solution)/shard_map/all_to_all | solution.py:112
  27.8 17.2 %copy-start.5 = (bf16[64,512]{1,0:T(8,128)(2,1)S(1)}, bf16[64,512]{1,0:T(8,128)(2,1)}, u32[]{:S(2)}) copy-start(bf16[64,512]{1,0:T(8,128)(2,1)} %param.21) | copy-start | bytes 196612
  27.8 17.9 %copy-start.8 = (s32[64,64]{1,0:T(8,128)S(1)}, s32[64,64]{1,0:T(8,128)}, u32[]{:S(2)}) copy-start(s32[64,64]{1,0:T(8,128)} %param.26) | copy-start | bytes 49156
  27.8 20.1 %copy-start.6 = (bf16[64,512]{1,0:T(8,128)(2,1)S(1)}, bf16[64,512]{1,0:T(8,128)(2,1)}, u32[]{:S(2)}) copy-start(bf16[64,512]{1,0:T(8,128)(2,1)} %param.22) | copy-start | bytes 196612
  27.8 20.8 %copy-start.12 = (f32[2,4]{1,0:T(2,128)S(1)}, f32[2,4]{1,0:T(2,128)}, u32[]{:S(2)}) copy-start(f32[2,4]{1,0:T(2,128)} %param.37) | copy-start | bytes 100
  29.4 11.7 %all-to-all-start.1 = ((f32[1,16,128]{2,0,1:T(1,128)}), f32[1,16,128]{2,0,1:T(1,128)S(1)}, u32[]{:S(2)}, u32[]{:S(2)}) async-start(f32[1,16,128]{2,0,1:T(1,128)} %bitcast.7), calls=%async_computation.1 | async-start | bytes 16384 | tf_op jit(solution)/shard_map/all_to_all | solution.py:109
  41.1 26.5 %all-to-all-start = ((f32[1,2048,128]{2,0,1:T(1,128)}), f32[1,2048,128]{2,0,1:T(1,128)S(1)}, u32[]{:S(2)}, u32[]{:S(2)}) async-start(f32[1,2048,128]{2,0,1:T(1,128)} %bitcast.5), calls=%async_computation | async-start | bytes 2097152 | tf_op jit(solution)/shard_map/all_to_all | solution.py:115
  44.8 72.7 %all-reduce.3.cloned.1.call-start = ((), (), s32[]{:S(2)}) async-start(), calls=%async_computation.4 | async-start | bytes 131072 | tf_op jit(solution)/shard_map/psum | solution.py:149
  92.5 5.1 %copy-start.4 = (bf16[4096,512]{1,0:T(8,128)(2,1)S(1)}, bf16[4096,512]{1,0:T(8,128)(2,1)}, u32[]{:S(2)}) copy-start(bf16[4096,512]{1,0:T(8,128)(2,1)} %param.28) | copy-start | bytes 12582916
  97.6 1.6 copy-start.7
  97.6 53.6 %copy-start.13 = (f32[512]{0:T(512)S(1)}, f32[512]{0:T(512)}, u32[]{:S(2)}) copy-start(f32[512]{0:T(512)} %param.30) | copy-start | bytes 6148
  99.1 86.8 %all-gather.2.cloned.1.call-start = ((), (), s32[]{:S(2)}) async-start(), calls=%async_computation.5 | async-start | bytes 1114112 | tf_op jit(solution)/shard_map/all_gather | solution.py:154
  152.8 124.9 %reduce-scatter.2.cloned.1.call-start = ((), (), s32[]{:S(2)}) async-start(), calls=%async_computation.6 | async-start | bytes 2228224 | tf_op jit(solution)/shard_map/reduce_scatter | solution.py:180
  185.9 9.2 %copy-start.2 = (bf16[64,8192]{1,0:T(8,128)(2,1)S(1)}, bf16[64,8192]{1,0:T(8,128)(2,1)}, u32[]{:S(2)}) copy-start(bf16[64,8192]{1,0:T(8,128)(2,1)} %all-gather.2.cloned.1.call-done) | copy-start | bytes 3145732
  185.9 18.1 %slice-start = ((s8[8388608]{0:T(1024)(128)(4,1)}), s8[4194304]{0:T(1024)(128)(4,1)S(1)}, s32[]{:S(2)}) async-start(s8[8388608]{0:T(1024)(128)(4,1)} %bitcast.95), calls=%async_computation.8 | async-start | bytes 8388608
  185.9 19.7 %slice-start.2 = ((s8[8388608]{0:T(1024)(128)(4,1)}), s8[4194304]{0:T(1024)(128)(4,1)S(1)}, s32[]{:S(2)}) async-start(s8[8388608]{0:T(1024)(128)(4,1)} %bitcast.97), calls=%async_computation.10 | async-start | bytes 8388608
  195.1 8.9 %slice-start.1 = ((s8[8388608]{0:T(1024)(128)(4,1)}), s8[4194304]{0:T(1024)(128)(4,1)S(1)}, s32[]{:S(2)}) async-start(s8[8388608]{0:T(1024)(128)(4,1)} %bitcast.95), calls=%async_computation.9 | async-start | bytes 8388608
  195.1 10.5 %slice-start.3 = ((s8[8388608]{0:T(1024)(128)(4,1)}), s8[4194304]{0:T(1024)(128)(4,1)S(1)}, s32[]{:S(2)}) async-start(s8[8388608]{0:T(1024)(128)(4,1)} %bitcast.97), calls=%async_computation.11 | async-start | bytes 8388608
  204.0 3.2 %slice-start.6 = ((s8[16777216]{0:T(1024)(128)(4,1)}), s8[4194304]{0:T(1024)(128)(4,1)S(1)}, s32[]{:S(2)}) async-start(s8[16777216]{0:T(1024)(128)(4,1)} %bitcast.102), calls=%async_computation.14 | async-start | bytes 8388608
  204.0 3.5 %slice-start.7 = ((s8[16777216]{0:T(1024)(128)(4,1)}), s8[4194304]{0:T(1024)(128)(4,1)S(1)}, s32[]{:S(2)}) async-start(s8[16777216]{0:T(1024)(128)(4,1)} %bitcast.102), calls=%async_computation.15 | async-start | bytes 8388608
  204.0 4.6 %slice-start.8 = ((s8[16777216]{0:T(1024)(128)(4,1)}), s8[4194304]{0:T(1024)(128)(4,1)S(1)}, s32[]{:S(2)}) async-start(s8[16777216]{0:T(1024)(128)(4,1)} %bitcast.102), calls=%async_computation.16 | async-start | bytes 8388608
  205.6 4.4 %slice-start.9 = ((s8[16777216]{0:T(1024)(128)(4,1)}), s8[4194304]{0:T(1024)(128)(4,1)S(1)}, s32[]{:S(2)}) async-start(s8[16777216]{0:T(1024)(128)(4,1)} %bitcast.102), calls=%async_computation.17 | async-start | bytes 8388608
  205.6 7.4 %slice-start.4 = ((s8[8388608]{0:T(1024)(128)(4,1)}), s8[4194304]{0:T(1024)(128)(4,1)S(1)}, s32[]{:S(2)}) async-start(s8[8388608]{0:T(1024)(128)(4,1)} %bitcast.99), calls=%async_computation.12 | async-start | bytes 8388608
  210.1 3.0 slice-start.5
  213.1 86.6 %copy-start.11 = (bf16[64,512]{1,0:T(8,128)(2,1)S(1)}, bf16[64,512]{1,0:T(8,128)(2,1)}, u32[]{:S(2)}) copy-start(bf16[64,512]{1,0:T(8,128)(2,1)} %all-reduce.3.cloned.1.call-done) | copy-start | bytes 196612
  213.1 88.8 %copy-start.1 = (bf16[64,4096]{1,0:T(8,128)(2,1)S(1)}, bf16[64,4096]{1,0:T(8,128)(2,1)}, u32[]{:S(2)}) copy-start(bf16[64,4096]{1,0:T(8,128)(2,1)} %param.20) | copy-start | bytes 1572868
  216.1 83.7 %all-reduce.5.cloned.1.call-start = ((), (), s32[]{:S(2)}) async-start(), calls=%async_computation.7 | async-start | bytes 131072 | tf_op jit(solution)/shard_map/psum | solution.py:186
Sparse Core Ops, SparseCore 0:
  99.3 18.2 all-reduce.2
  152.9 32.9 all-gather.1
  216.2 61.4 reduce-scatter.1
  279.8 19.8 all-reduce.4
where the time goes:
time: 309 us; the launch traced here: 308 us
  waiting for transfers between devices  154 us (50%)
  blocking collectives  56.7 us (18%)
  matrix products  39 us (13%)
  starting transfers between devices  16.6 us (5%)
  local copies, waits for them, and re-layouts  16.5 us (5%)
  between operations  13.7 us (4%)
  other arithmetic  12.1 us (4%)
    reduce_scatter x1, waiting for transfers between devices, shards(): lax.psum_scatter(base_part + delta_part.reshape(features_here * lax.axis_...  59.5 us
    all_gather x1, waiting for transfers between devices, shards(): piece = lax.all_gather(normed, 'ctx', axis=1, tiled=True)  32.9 us
    psum x1, blocking collectives, shards(): squares = lax.psum(jnp.sum(hidden * hidden, axis=1), 'ctx')  32.7 us
    all_gather x1, blocking collectives, shards(): lax.all_gather(finished, 'ctx', axis=0, tiled=True)  24 us
    psum x1, waiting for transfers between devices, shards(): lowered = lax.psum(lowered.astype(jnp.bfloat16), 'kv').astype(jnp.float32)  20.4 us
    psum x1, waiting for transfers between devices, shards(): lax.psum(projected.astype(jnp.bfloat16), 'kv').astype(jnp.float32)  17.6 us
    all_to_all x1, waiting for transfers between devices, shards(): lax.all_to_all(part_out.reshape(1, all_rows, HEAD_SIZE), 'ctx', split_axi...  17.5 us
    dot_general x1, matrix products, shards(): jnp.einsum('tqf,tfh->tqh', split_piece, gate_signs, preferred_element_typ...  9.14 us
  transfers between devices with their start and end apart: 7, of which 7 were waited for; matrix products, arithmetic and copies ran while one was open for 5% of the time, Pallas kernels for 0%

commit v1 on v0

--- a/solution.py
+++ b/solution.py
@@ -63,6 +63,11 @@
     down_signs,
     delta_scale,
 ):
+
+    def review_files(slab_in, ndim_at=1):
+        y = jnp.concatenate(lax.all_gather(slab_in, axis_name="ctx"), axis=ndim_at)
+        return y
+
     tenants = cache_keys.shape[0]
     tokens = tenant_ids.shape[0]
     draft = tokens // tenants
@@ -151,7 +156,7 @@
     squares = lax.psum(jnp.sum(hidden * hidden, axis=1), "ctx")
     normed = (hidden * lax.rsqrt(squares / D + EPS)[:, None] * norm_gain).astype(jnp.bfloat16)
     hidden_units = gate_weight.shape[1]
-    piece = lax.all_gather(normed, "ctx", axis=1, tiled=True)
+    piece = review_files(normed)
     size = piece.shape[1]
     split_piece = piece.reshape(tenants, draft, size)
     gate_base = jnp.dot(piece, gate_weight, preferred_element_type=jnp.float32)

time: 309 us -> 314 us (1.016)
  local copies, waits for them, and re-layouts: 16.5 us -> 21.1 us
  transfers between devices with their start and end apart: 7 -> 7, of which waited for: 7 -> 7; matrix products, arithmetic and copies ran while one was open for 5% -> 4% of each run, Pallas kernels for 0% -> 0%
where the time goes in v1:
time: 314 us; the launch traced here: 313 us
  waiting for transfers between devices  154 us (49%)
  blocking collectives  56.7 us (18%)
  matrix products  38.7 us (12%)
  local copies, waits for them, and re-layouts  21.1 us (7%)
  starting transfers between devices  16.6 us (5%)
  between operations  13.7 us (4%)
  other arithmetic  12.1 us (4%)
    reduce_scatter x1, waiting for transfers between devices, shards(): lax.psum_scatter(base_part + delta_part.reshape(features_here * lax.axis_...  58.9 us
    all_gather x1, waiting for transfers between devices, review_files(): y = jnp.concatenate(lax.all_gather(slab_in, axis_name='ctx'), axis=ndim_at)  34.1 us
    psum x1, blocking collectives, shards(): squares = lax.psum(jnp.sum(hidden * hidden, axis=1), 'ctx')  32.7 us
    all_gather x1, blocking collectives, shards(): lax.all_gather(finished, 'ctx', axis=0, tiled=True)  24 us
    psum x1, waiting for transfers between devices, shards(): lowered = lax.psum(lowered.astype(jnp.bfloat16), 'kv').astype(jnp.float32)  20.4 us
    psum x1, waiting for transfers between devices, shards(): lax.psum(projected.astype(jnp.bfloat16), 'kv').astype(jnp.float32)  17.6 us
    all_to_all x1, waiting for transfers between devices, shards(): lax.all_to_all(part_out.reshape(1, all_rows, HEAD_SIZE), 'ctx', split_axi...  17.5 us
    dot_general x1, matrix products, shards(): jnp.einsum('tqf,tfh->tqh', split_piece, gate_signs, preferred_element_typ...  8.82 us
  transfers between devices with their start and end apart: 7, of which 7 were waited for; matrix products, arithmetic and copies ran while one was open for 4% of the time, Pallas kernels for 0%

profile of v1, /device:TPU:0, one launch (start us, length us, event | category | flops | bytes accessed | tf_op | source)
XLA Modules:
  0.0 313.3 jit_solution(4109980580644726731)
XLA Ops:
  6.5 2.8 sort.34
  9.4 0.9 gather_fusion.1
  10.7 0.9 bitcast_reduce_fusion
  11.7 1.9 copy-done.2
  13.6 1.3 fusion.3
  14.9 0.8 all_to_all.38
  15.7 7.4 %all-to-all-start.2 = ((f32[1,16,128]{2,0,1:T(1,128)}), f32[1,16,128]{2,0,1:T(1,128)S(1)}, u32[]{:S(2)}, u32[]{:S(2)}) async-start(f32[1,16,128]{2,0,1:T(1,128)} %bitcast.17), calls=%async_computation.2 | async-start | bytes 16384 | tf_op jit(solution)/shard_map/all_to_all | solution.py:117
  23.1 1.1 reshape.254
  24.2 3.6 %fusion.9 = f32[2,32,4,8,128]{4,3,1,2,0:T(8,128)S(1)} fusion(f32[2,4,32,8,512]{4,3,2,1,0:T(8,128)} %copy-done.2, f32[2,32,4,8]{3,1,2,0:T(8,128)S(1)} %get-tuple-element.20, pred[2,512]{1,0:T(4,128)(4,1)S(1)} %broadcast_compare_fusion, bf16[2,512,4,128,1]{3,2,1,0,4:T(4,128)(2,1)} %bitcast.122), kind=kOutput, calls=%fused_computation.21 | convolution fusion | flops 273678336 | bytes 6300672 | tf_op jit(solution)/shard_map/tqgwj,tjgd->tqgwd/dot_general | solution.py:101
  27.9 0.7 all_to_all.35
  28.7 0.8 all-to-all-done.2
  29.4 5.2 %all-to-all-start.1 = ((f32[1,16,128]{2,0,1:T(1,128)}), f32[1,16,128]{2,0,1:T(1,128)S(1)}, u32[]{:S(2)}, u32[]{:S(2)}) async-start(f32[1,16,128]{2,0,1:T(1,128)} %bitcast.7), calls=%async_computation.1 | async-start | bytes 16384 | tf_op jit(solution)/shard_map/all_to_all | solution.py:114
  35.0 1.1 copy.52
  36.1 5.0 %all-to-all-done.1 = f32[1,16,128]{2,0,1:T(1,128)S(1)} async-done(((f32[1,16,128]{2,0,1:T(1,128)}), f32[1,16,128]{2,0,1:T(1,128)S(1)}, u32[]{:S(2)}, u32[]{:S(2)}) %all-to-all-start.1) | async-done | bytes 8224 | tf_op jit(solution)/shard_map/all_to_all | solution.py:114
  41.1 3.7 %all-to-all-start = ((f32[1,2048,128]{2,0,1:T(1,128)}), f32[1,2048,128]{2,0,1:T(1,128)S(1)}, u32[]{:S(2)}, u32[]{:S(2)}) async-start(f32[1,2048,128]{2,0,1:T(1,128)} %bitcast.5), calls=%async_computation | async-start | bytes 2097152 | tf_op jit(solution)/shard_map/all_to_all | solution.py:120
  45.0 0.7 gather_fusion.5
  45.7 0.6 gather_fusion.2
  46.4 0.6 gather_fusion.3
  47.2 0.7 gather_fusion.4
  47.9 0.7 gather_fusion.6
  49.3 0.7 fusion.22
  50.1 17.5 %all-to-all-done = f32[1,2048,128]{2,0,1:T(1,128)S(1)} async-done(((f32[1,2048,128]{2,0,1:T(1,128)}), f32[1,2048,128]{2,0,1:T(1,128)S(1)}, u32[]{:S(2)}, u32[]{:S(2)}) %all-to-all-start) | async-done | bytes 1048608 | tf_op jit(solution)/shard_map/all_to_all | solution.py:120
  67.6 0.3 multiply_reduce_fusion
  68.1 24.0 %all_gather.9 = bf16[2048,128]{1,0:T(8,128)(2,1)S(1)} all-gather(bf16[128,128]{1,0:T(8,128)(2,1)S(1)} %divide_convert_fusion), channel_id=1, replica_groups=mesh['kv'=2,'ctx'=16] {'ctx'}, dimensions={0}, use_global_device_ids=true | all-gather | bytes 557056 | tf_op jit(solution)/shard_map/all_gather | solution.py:143
  92.6 5.1 %convolution_multiply_fusion.1 = f32[2,32,512]{2,1,0:T(8,128)S(1)} fusion(bf16[2,32,4096]{2,1,0:T(8,128)(2,1)S(1)} %reshape_reshape.12, bf16[2,4096,512]{2,1,0:T(8,128)(2,1)} %param.29, f32[2]{0:T(128)S(1)} %get-tuple-element.11), kind=kOutput, calls=%fused_computation.22 | convolution fusion | flops 268468224 | bytes 9043976 | tf_op jit(solution)/shard_map/tqh,thf->tqf/dot_general | solution.py:148
  97.6 1.5 fusion.16
  99.2 0.7 gather_fusion
  99.9 17.6 %all-reduce.3.cloned.1.call-done = bf16[64,512]{1,0:T(8,128)(2,1)} async-done(((bf16[64,512]{1,0:T(8,128)(2,1)}), bf16[64,512]{1,0:T(8,128)(2,1)}) %all-reduce.3.cloned.1.call-update) | async-done | bytes 65552 | tf_op jit(solution)/shard_map/psum | solution.py:154
  117.5 1.0 multiply_reduce_fusion.1
  118.5 32.7 %psum.22 = f32[64]{0:T(128)S(1)} all-reduce(f32[64]{0:T(128)S(1)} %multiply_reduce_fusion.1), channel_id=1, replica_groups=mesh['kv'=2,'ctx'=16] {'ctx'}, use_global_device_ids=true, to_apply=%region_10.11 | all-reduce | flops 64 | bytes 512 | tf_op jit(solution)/shard_map/psum | solution.py:156
  151.2 1.6 multiply_convert_fusion
  153.0 34.1 %all-gather.3.cloned.1.call-done = bf16[1024,512]{1,0:T(8,128)(2,1)} async-done(((bf16[64,512]{1,0:T(8,128)(2,1)}), bf16[1024,512]{1,0:T(8,128)(2,1)}) %all-gather.3.cloned.1.call-update) | async-done | bytes 1048592 | tf_op jit(solution)/shard_map/all_gather | solution.py:68
  187.1 2.9 copy.109
  190.0 1.6 reshape_reshape.13
  191.7 8.8 %convolution_multiply_fusion.3 = f32[2,32,512]{2,1,0:T(8,128)S(1)} fusion(bf16[2,32,8192]{2,1,0:T(8,128)(2,1)S(1)} %reshape_reshape.13, bf16[2,8192,512]{2,1,0:T(8,128)(2,1)} %param.34, f32[2]{0:T(128)S(1)} %get-tuple-element.10), kind=kOutput, calls=%fused_computation.27 | convolution fusion | flops 536903680 | bytes 17956872 | tf_op jit(solution)/shard_map/tqf,tfh->tqh/dot_general | solution.py:164
  200.6 8.8 %convolution_multiply_fusion.2 = f32[2,32,512]{2,1,0:T(8,128)S(1)} fusion(bf16[2,32,8192]{2,1,0:T(8,128)(2,1)S(1)} %reshape_reshape.13, bf16[2,8192,512]{2,1,0:T(8,128)(2,1)} %param.35, f32[2]{0:T(128)S(1)} %get-tuple-element.12), kind=kOutput, calls=%fused_computation.24 | convolution fusion | flops 536903680 | bytes 17956872 | tf_op jit(solution)/shard_map/tqf,tfh->tqh/dot_general | solution.py:167
  209.5 1.6 convolution_add_fusion.2
  211.1 1.6 fusion.15
  212.9 1.2 slice-done.8
  214.1 1.4 slice-done.9
  215.5 3.0 convolution_multiply_fusion
  218.6 2.9 fusion
  221.6 2.0 sort.35
  223.6 58.9 %reduce-scatter.2.cloned.1.call-done = f32[512,64]{0,1:T(8,128)} async-done(((f32[8192,64]{0,1:T(8,128)}), f32[512,64]{0,1:T(8,128)}) %reduce-scatter.2.cloned.1.call-update) | async-done | bytes 131088 | tf_op jit(solution)/shard_map/reduce_scatter | solution.py:185
  282.5 1.5 convert_bitcast_fusion
  284.1 20.4 %all-reduce.5.cloned.1.call-done = bf16[64,512]{1,0:T(8,128)(2,1)} async-done(((bf16[64,512]{1,0:T(8,128)(2,1)}), bf16[64,512]{1,0:T(8,128)(2,1)}) %all-reduce.5.cloned.1.call-update) | async-done | bytes 65552 | tf_op jit(solution)/shard_map/psum | solution.py:191
  304.5 0.9 add_convert_fusion
  305.4 1.3 gather_fusion.7
  (94 shorter events, 3.6 us)
Async XLA Ops:
  6.5 2.8 copy-start
  6.5 3.8 %copy-start.9 = (bf16[2,512,512]{2,1,0:T(8,128)(2,1)S(1)}, bf16[2,512,512]{2,1,0:T(8,128)(2,1)}, u32[]{:S(2)}) copy-start(bf16[2,512,512]{2,1,0:T(8,128)(2,1)} %param.23) | copy-start | bytes 3145732
  6.5 4.1 %copy-start.14 = (s32[2]{0:T(128)S(1)}, s32[2]{0:T(128)}, u32[]{:S(2)}) copy-start(s32[2]{0:T(128)} %param.27) | copy-start | bytes 28
  10.7 12.3 %copy-start.10 = (bf16[2,512,512]{2,1,0:T(8,128)(2,1)S(1)}, bf16[2,512,512]{2,1,0:T(8,128)(2,1)}, u32[]{:S(2)}) copy-start(bf16[2,512,512]{2,1,0:T(8,128)(2,1)} %param.24) | copy-start | bytes 3145732
  11.6 1.9 copy-start.2
  15.7 13.8 %all-to-all-start.2 = ((f32[1,16,128]{2,0,1:T(1,128)}), f32[1,16,128]{2,0,1:T(1,128)S(1)}, u32[]{:S(2)}, u32[]{:S(2)}) async-start(f32[1,16,128]{2,0,1:T(1,128)} %bitcast.17), calls=%async_computation.2 | async-start | bytes 16384 | tf_op jit(solution)/shard_map/all_to_all | solution.py:117
  27.8 17.2 %copy-start.5 = (bf16[64,512]{1,0:T(8,128)(2,1)S(1)}, bf16[64,512]{1,0:T(8,128)(2,1)}, u32[]{:S(2)}) copy-start(bf16[64,512]{1,0:T(8,128)(2,1)} %param.21) | copy-start | bytes 196612
  27.8 17.9 %copy-start.8 = (s32[64,64]{1,0:T(8,128)S(1)}, s32[64,64]{1,0:T(8,128)}, u32[]{:S(2)}) copy-start(s32[64,64]{1,0:T(8,128)} %param.26) | copy-start | bytes 49156
  27.8 20.1 %copy-start.6 = (bf16[64,512]{1,0:T(8,128)(2,1)S(1)}, bf16[64,512]{1,0:T(8,128)(2,1)}, u32[]{:S(2)}) copy-start(bf16[64,512]{1,0:T(8,128)(2,1)} %param.22) | copy-start | bytes 196612
  27.8 20.8 %copy-start.12 = (f32[2,4]{1,0:T(2,128)S(1)}, f32[2,4]{1,0:T(2,128)}, u32[]{:S(2)}) copy-start(f32[2,4]{1,0:T(2,128)} %param.37) | copy-start | bytes 100
  29.4 11.7 %all-to-all-start.1 = ((f32[1,16,128]{2,0,1:T(1,128)}), f32[1,16,128]{2,0,1:T(1,128)S(1)}, u32[]{:S(2)}, u32[]{:S(2)}) async-start(f32[1,16,128]{2,0,1:T(1,128)} %bitcast.7), calls=%async_computation.1 | async-start | bytes 16384 | tf_op jit(solution)/shard_map/all_to_all | solution.py:114
  41.1 26.5 %all-to-all-start = ((f32[1,2048,128]{2,0,1:T(1,128)}), f32[1,2048,128]{2,0,1:T(1,128)S(1)}, u32[]{:S(2)}, u32[]{:S(2)}) async-start(f32[1,2048,128]{2,0,1:T(1,128)} %bitcast.5), calls=%async_computation | async-start | bytes 2097152 | tf_op jit(solution)/shard_map/all_to_all | solution.py:120
  44.8 72.7 %all-reduce.3.cloned.1.call-start = ((), (), s32[]{:S(2)}) async-start(), calls=%async_computation.4 | async-start | bytes 131072 | tf_op jit(solution)/shard_map/psum | solution.py:154
  92.5 5.1 %copy-start.3 = (bf16[4096,512]{1,0:T(8,128)(2,1)S(1)}, bf16[4096,512]{1,0:T(8,128)(2,1)}, u32[]{:S(2)}) copy-start(bf16[4096,512]{1,0:T(8,128)(2,1)} %param.28) | copy-start | bytes 12582916
  97.6 1.6 copy-start.7
  97.6 53.6 %copy-start.13 = (f32[512]{0:T(512)S(1)}, f32[512]{0:T(512)}, u32[]{:S(2)}) copy-start(f32[512]{0:T(512)} %param.30) | copy-start | bytes 6148
  99.1 87.9 %all-gather.3.cloned.1.call-start = ((), (), s32[]{:S(2)}) async-start(), calls=%async_computation.7 | async-start | bytes 1114112 | tf_op jit(solution)/shard_map/all_gather | solution.py:68
  152.8 129.8 %reduce-scatter.2.cloned.1.call-start = ((), (), s32[]{:S(2)}) async-start(), calls=%async_computation.5 | async-start | bytes 2228224 | tf_op jit(solution)/shard_map/reduce_scatter | solution.py:185
  187.1 4.5 %copy-start.4 = (bf16[1024,512]{1,0:T(8,128)(2,1)S(1)}, bf16[1024,512]{1,0:T(8,128)(2,1)}, u32[]{:S(2)}) copy-start(bf16[1024,512]{1,0:T(8,128)(2,1)} %all-gather.3.cloned.1.call-done) | copy-start | bytes 3145732
  191.7 17.8 %slice-start = ((s8[8388608]{0:T(1024)(128)(4,1)}), s8[4194304]{0:T(1024)(128)(4,1)S(1)}, s32[]{:S(2)}) async-start(s8[8388608]{0:T(1024)(128)(4,1)} %bitcast.100), calls=%async_computation.8 | async-start | bytes 8388608
  191.7 19.4 %slice-start.2 = ((s8[8388608]{0:T(1024)(128)(4,1)}), s8[4194304]{0:T(1024)(128)(4,1)S(1)}, s32[]{:S(2)}) async-start(s8[8388608]{0:T(1024)(128)(4,1)} %bitcast.102), calls=%async_computation.10 | async-start | bytes 8388608
  200.5 8.9 %slice-start.1 = ((s8[8388608]{0:T(1024)(128)(4,1)}), s8[4194304]{0:T(1024)(128)(4,1)S(1)}, s32[]{:S(2)}) async-start(s8[8388608]{0:T(1024)(128)(4,1)} %bitcast.100), calls=%async_computation.9 | async-start | bytes 8388608
  200.6 10.5 %slice-start.3 = ((s8[8388608]{0:T(1024)(128)(4,1)}), s8[4194304]{0:T(1024)(128)(4,1)S(1)}, s32[]{:S(2)}) async-start(s8[8388608]{0:T(1024)(128)(4,1)} %bitcast.102), calls=%async_computation.11 | async-start | bytes 8388608
  209.5 3.2 %slice-start.6 = ((s8[16777216]{0:T(1024)(128)(4,1)}), s8[4194304]{0:T(1024)(128)(4,1)S(1)}, s32[]{:S(2)}) async-start(s8[16777216]{0:T(1024)(128)(4,1)} %bitcast.109), calls=%async_computation.14 | async-start | bytes 8388608
  209.5 3.5 %slice-start.7 = ((s8[16777216]{0:T(1024)(128)(4,1)}), s8[4194304]{0:T(1024)(128)(4,1)S(1)}, s32[]{:S(2)}) async-start(s8[16777216]{0:T(1024)(128)(4,1)} %bitcast.109), calls=%async_computation.15 | async-start | bytes 8388608
  209.5 4.6 %slice-start.8 = ((s8[16777216]{0:T(1024)(128)(4,1)}), s8[4194304]{0:T(1024)(128)(4,1)S(1)}, s32[]{:S(2)}) async-start(s8[16777216]{0:T(1024)(128)(4,1)} %bitcast.109), calls=%async_computation.16 | async-start | bytes 8388608
  211.1 4.4 %slice-start.9 = ((s8[16777216]{0:T(1024)(128)(4,1)}), s8[4194304]{0:T(1024)(128)(4,1)S(1)}, s32[]{:S(2)}) async-start(s8[16777216]{0:T(1024)(128)(4,1)} %bitcast.109), calls=%async_computation.17 | async-start | bytes 8388608
  211.1 7.4 %slice-start.4 = ((s8[8388608]{0:T(1024)(128)(4,1)}), s8[4194304]{0:T(1024)(128)(4,1)S(1)}, s32[]{:S(2)}) async-start(s8[8388608]{0:T(1024)(128)(4,1)} %bitcast.106), calls=%async_computation.12 | async-start | bytes 8388608
  215.5 3.0 slice-start.5
  218.6 86.0 %copy-start.11 = (bf16[64,512]{1,0:T(8,128)(2,1)S(1)}, bf16[64,512]{1,0:T(8,128)(2,1)}, u32[]{:S(2)}) copy-start(bf16[64,512]{1,0:T(8,128)(2,1)} %all-reduce.3.cloned.1.call-done) | copy-start | bytes 196612
  218.6 88.2 %copy-start.1 = (bf16[64,4096]{1,0:T(8,128)(2,1)S(1)}, bf16[64,4096]{1,0:T(8,128)(2,1)}, u32[]{:S(2)}) copy-start(bf16[64,4096]{1,0:T(8,128)(2,1)} %param.20) | copy-start | bytes 1572868
  221.5 83.0 %all-reduce.5.cloned.1.call-start = ((), (), s32[]{:S(2)}) async-start(), calls=%async_computation.6 | async-start | bytes 131072 | tf_op jit(solution)/shard_map/psum | solution.py:191
Sparse Core Ops, SparseCore 0:
  99.3 18.2 all-reduce.2
  152.9 34.1 all-gather.2
  221.6 60.8 reduce-scatter.1
  284.6 19.8 all-reduce.4
